TPU v7x, 32 devices: a whole 2x2x4 slice. The times are simulated.
32 devices in a mesh: grp: 16 (over z, y, core), sub: 2 (over x).
Axes of the slice: x: 2, y: 2, z: 4, core: 2. Of those that a mesh axis runs over, the one named last changes fastest.
Arguments:
- state_zero: float32 [352, 16807], P(('grp', 'sub')), as said below
- state_one: float32 [224, 7776], P(('grp', 'sub')), as said below
- state_two: float32 [224, 7776], P(('grp', 'sub')), as said below
- state_three: float32 [128, 3125], P(('grp', 'sub')), as said below
- intra_zero: float32 [8, 7, 7], replicated, may hold values from -0.75 to 0.75
- intra_one: float32 [8, 6, 6], replicated, may hold values from -0.875 to 0.875
- intra_two: float32 [8, 6, 6], replicated, may hold values from -0.875 to 0.875
- intra_three: float32 [8, 5, 5], replicated, may hold values from -1 to 1
- intersections: float32 [3, 8, 7, 7], replicated, may hold values from -2 to 2
- positions: float32 [3, 8, 7, 7], replicated, may hold values from -2 to 2
- coupling_pair: int32 [24], replicated, may hold values from 0 to 2
- coupling_mode: int32 [24], replicated, may hold values from 0 to 7
- coupling_strength: float32 [24], replicated, may hold values from -3 to 3
Outputs:
- stepped_zero: float32 [352, 16807], P(('grp', 'sub'))
- stepped_one: float32 [224, 7776], P(('grp', 'sub'))
- stepped_two: float32 [224, 7776], P(('grp', 'sub'))
- stepped_three: float32 [128, 3125], P(('grp', 'sub'))
- density_zero: float32 [8, 7, 7], replicated
- density_one: float32 [8, 6, 6], replicated
- density_two: float32 [8, 6, 6], replicated
- density_three: float32 [8, 5, 5], replicated
Inputs may be any that keep to these rules, and one draw needn't show every extreme that they name: `state_zero`: rows from 7**3 on are zero. `state_one`: rows from 6**3 on are zero. `state_two`: rows from 6**3 on are zero. `state_three`: rows from 5**3 on are zero.
All inputs are finite; a program needn't handle non-finite values.
Results may differ from a plain program's by a relative error of at most 0.0001.
Values sent between devices are 32-bit elements; how exact they have to be, the bound alone decides.
A program may use at most 256 MiB of HBM per device.

v0:
```python
import functools
import math

import jax
import jax.numpy as jnp
import numpy as np
from jax import lax
from jax.experimental import pallas as pl
from jax.experimental.pallas import tpu as pltpu
from jax.sharding import PartitionSpec as P

highest = lax.Precision.HIGHEST
time_step = 0.25
lanes = 128
vmem_limit = 63 * 1024 * 1024
params = pltpu.CompilerParams(vmem_limit_bytes=vmem_limit)
vmem = pl.BlockSpec(memory_space=pltpu.VMEM)
mesh_ids = pl.DeviceIdType.MESH


def digits(width, count, total, place):
    index = np.arange(total)
    live = index < width**count
    digit = (index // width ** (count - 1 - place)) % width
    return ((digit[None, :] == np.arange(width)[:, None]) & live[None, :]).astype(np.float32)


def others(width, count, total, place):
    index = np.arange(total)
    stride = width ** (count - 1 - place)
    rest = index - ((index // stride) % width) * stride
    return np.where(index < width**count, rest, -1).astype(np.int32)


def split(value):
    top = value.astype(jnp.bfloat16)
    return top, (value - top.astype(jnp.float32)).astype(jnp.bfloat16)


def dot3(left, right, contract):
    dims = (contract, ((), ()))
    go = functools.partial(lax.dot_general, dimension_numbers=dims, preferred_element_type=jnp.float32)
    return go(left[0], right[0]) + (go(left[0], right[1]) + go(left[1], right[0]))


def pack_kernel(plan, *refs):
    count = len(plan)
    for source, out, (rows, columns, tiles) in zip(refs[:count], refs[count:], plan):
        used = tiles * rows
        if out.shape[1] > used:
            out[:, used:, :] = jnp.zeros((out.shape[0], out.shape[1] - used, lanes), jnp.float32)
        for device in range(out.shape[0]):
            for tile in range(tiles):
                start = (device * tiles + tile) * lanes
                width = min(lanes, columns - start)
                at = slice(tile * rows, (tile + 1) * rows)
                if width < lanes:
                    out[device, at, :] = jnp.zeros((rows, lanes), jnp.float32)
                if width > 0:
                    out[device, at, :width] = source[:, start : start + width]


def flow_kernel(plan, combos, layers, wide, *refs):
    count = len(plan)
    spare = list(refs)

    def take(number):
        taken = spare[:number]
        del spare[:number]
        return taken

    sends, states = take(count), take(count)
    small, scalars = take(2)
    kinds = [item["kind"] for item in plan]
    tables = [take(max(kinds) + 1) for _ in range(8)]
    lead_pick, lead_turned, lead_rest, lead_rest_turned, tail_pick, tail_turned, tail_rest, tail_rest_turned = [
        [table[kind] for kind in kinds] for table in tables
    ]
    stepped, densities = take(count), take(count)
    gathered, mixed, back = take(count), take(count), take(count)
    value, result = take(2)
    matrices = [take(len(item["targets"])) for item in plan]
    tails = {key: take(1 if key[0] == key[1] else 2) for key in combos}
    cubes, totals = take(count), take(count)
    zero_in, one_in, zero_out, one_out = take(4)
    inner_over, inner_pos, full_over, full_pos = take(4)
    sums, stage, layer_sums, rows_of_sums = take(4)
    across_send, across_recv, up_send, up_recv, down_send, down_recv, home_send, home_recv, own, sum_send, sum_recv = spare

    sub = lax.axis_size("sub")
    me = lax.axis_index("grp") * sub + lax.axis_index("sub")
    layer, place = me // wide, me % wide

    def device(at_layer, at_place):
        index = at_layer * wide + at_place
        return (index // sub, index % sub)

    def peer(step):
        return lax.rem(place + step, wide)

    def across(t, step):
        return pltpu.make_async_remote_copy(
            src_ref=sends[t].at[peer(step)],
            dst_ref=gathered[t].at[layer, place],
            send_sem=across_send.at[t, step],
            recv_sem=across_recv.at[t, step],
            device_id=device(layer, peer(step)),
            device_id_type=mesh_ids,
        )

    def home(t, step):
        return pltpu.make_async_remote_copy(
            src_ref=mixed[t].at[peer(step)],
            dst_ref=back[t].at[place],
            send_sem=home_send.at[t, step],
            recv_sem=home_recv.at[t, step],
            device_id=device(layer, peer(step)),
            device_id_type=mesh_ids,
        )

    def hop(t, step, up):
        block = layer - step if up else layer + step
        return pltpu.make_async_remote_copy(
            src_ref=gathered[t].at[block],
            dst_ref=gathered[t].at[block],
            send_sem=(up_send if up else down_send).at[t, step],
            recv_sem=(up_recv if up else down_recv).at[t, step],
            device_id=device(layer + 1 if up else layer - 1, place),
            device_id_type=mesh_ids,
        )

    def sends_hop(step, up):
        if up:
            return jnp.logical_and(layer - step >= 0, layer + 1 < layers)
        return jnp.logical_and(layer + step < layers, layer >= 1)

    def forward(t, step):
        for up in (True, False):
            @pl.when(sends_hop(step, up))
            def _():
                hop(t, step, up).start()

    def arrive(t, step):
        @pl.when(layer - 1 - step >= 0)
        def _():
            pltpu.make_async_remote_copy(
                src_ref=gathered[t].at[layer - 1 - step],
                dst_ref=gathered[t].at[layer - 1 - step],
                send_sem=up_send.at[t, step],
                recv_sem=up_recv.at[t, step],
                device_id=device(layer - 1, place),
                device_id_type=mesh_ids,
            ).wait_recv()

        @pl.when(layer + 1 + step < layers)
        def _():
            pltpu.make_async_remote_copy(
                src_ref=gathered[t].at[layer + 1 + step],
                dst_ref=gathered[t].at[layer + 1 + step],
                send_sem=down_send.at[t, step],
                recv_sem=down_recv.at[t, step],
                device_id=device(layer + 1, place),
                device_id_type=mesh_ids,
            ).wait_recv()

    def keep(t):
        return pltpu.make_async_copy(sends[t].at[place], gathered[t].at[layer, place], own.at[t])

    def keep_home(t):
        return pltpu.make_async_copy(mixed[t].at[place], back[t].at[place], own.at[count + t])

    def layer_ready(t):
        keep(t).wait()
        for step in range(1, wide):
            across(t, step).wait_recv()

    def put_density(t, mode, block):
        at = (t * 8 + mode) * 8
        sums[:, at : at + 8] = block

    def add_density(t, mode, gram, rest_rows, rest_columns, pick, turned):
        kept = split(jnp.where(rest_rows == rest_columns, gram, 0.0))
        chosen = pick.astype(jnp.bfloat16)
        dims = (((1,), (1,)), ((), ()))
        right = lax.dot_general(kept[0], chosen, dims, preferred_element_type=jnp.float32) + lax.dot_general(
            kept[1], chosen, dims, preferred_element_type=jnp.float32
        )
        block = lax.dot_general(
            turned, right, (((0,), (0,)), ((), ())), precision=highest, preferred_element_type=jnp.float32
        )
        put_density(t, mode, 0.5 * (block + block.T))

    def mix(t):
        item = plan[t]
        rows, slot, tiles = item["rows"], item["slot"], item["tiles"]
        depth = layers * wide * slot
        value[:depth, : tiles * lanes] = jnp.zeros((depth, tiles * lanes), jnp.float32)

        @pl.loop(0, layers)
        def _(at_layer):
            @pl.loop(0, wide)
            def _(at_place):
                base = pl.multiple_of((at_layer * wide + at_place) * slot, slot)
                for tile in range(tiles):
                    value[pl.ds(base, rows), tile * lanes : (tile + 1) * lanes] = gathered[t][
                        at_layer, at_place, tile * rows : (tile + 1) * rows, :
                    ]

        blocks = []
        for matrix in matrices[t]:
            blocks.append(split(matrix[...]))
        mine = pl.ds(pl.multiple_of(layer * wide * slot, 8), wide * slot)
        gram = None
        for start in range(0, tiles, 2):
            wide_tiles = min(2, tiles - start)
            span = slice(start * lanes, (start + wide_tiles) * lanes)
            data = split(value[:depth, span])
            own_rows = split(value[mine, span])
            part = lax.dot_general(
                own_rows[0], data[0], (((1,), (1,)), ((), ())), preferred_element_type=jnp.float32
            ) + 2.0 * lax.dot_general(
                own_rows[0], data[1], (((1,), (1,)), ((), ())), preferred_element_type=jnp.float32
            )
            gram = part if gram is None else gram + part
            offset = 0
            for block, target in zip(blocks, item["targets"]):
                size = target * wide
                result[:size, : wide_tiles * lanes] = dot3(block, data, ((1,), (0,)))
                for at_place in range(wide):
                    for tile in range(wide_tiles):
                        row = offset + (start + tile) * target
                        mixed[t][at_place, row : row + target, :] = result[
                            at_place * target : (at_place + 1) * target, tile * lanes : (tile + 1) * lanes
                        ]
                offset += target * tiles
        if mixed[t].shape[1] > offset:
            mixed[t][:, offset:, :] = jnp.zeros((wide, mixed[t].shape[1] - offset, lanes), jnp.float32)
        for k in range(3):
            turned = lead_turned[t][k, mine, :]
            add_density(t, k, gram, lead_rest_turned[t][mine, k : k + 1], lead_rest[t][k : k + 1, :], lead_pick[t][k], turned)

    def send_home(t):
        keep_home(t).start()
        for step in range(1, wide):
            home(t, step).start()

    def expand(key, kind, mode, pick):
        matrix = small[(combos[key] * 2 + kind) * 8 + mode]
        out = None
        for b in range(plan[key[1]]["width"]):
            term = matrix[:, b : b + 1] * pick[b : b + 1, :]
            out = term if out is None else out + term
        return out

    def build(key, picks, mode, over_out, pos_out, rows):
        width = plan[key[0]]["width"]
        cols = picks.shape[-1]
        over = [expand(key, 0, mode + k, picks[k]) for k in range(3)]
        pos = [expand(key, 1, mode + k, picks[k]) for k in range(3)]
        square = width * width
        if rows > square * width:
            for out in (over_out, pos_out):
                if out is not None:
                    out[square * width : rows, :cols] = jnp.zeros((rows - square * width, cols), jnp.float32)
        for a in range(width):
            span = slice(a * width, (a + 1) * width)
            inner_over[span, :cols] = over[1][a : a + 1] * over[2][:width]
            inner_pos[span, :cols] = pos[1][a : a + 1] * over[2][:width] + over[1][a : a + 1] * pos[2][:width]
        over_value = inner_over[:square, :cols]
        pos_value = inner_pos[:square, :cols]
        for a in range(width):
            span = slice(a * square, (a + 1) * square)
            pos_out[span, :cols] = pos[0][a : a + 1] * over_value + over[0][a : a + 1] * pos_value
            if over_out is not None:
                over_out[span, :cols] = over[0][a : a + 1] * over_value

    def build_leads(t):
        cols = plan[t]["slot"] * layers * wide
        sources = [t] + [s for s in (t - 1, t + 1) if 0 <= s < count]
        at = 0
        for s in sources:
            rows = plan[s]["rows"]
            build((s, t), lead_pick[t], 0, full_over if s != t else None, full_pos, rows * layers * wide)
            mine = pl.ds(pl.multiple_of(layer * rows * wide, 8), rows * wide)
            for full in (full_over, full_pos) if s != t else (full_pos,):
                matrices[t][at][...] = full[mine, :cols]
                at += 1

    def build_tail(s, t):
        outs = tails[(s, t)]
        build((t, s), tail_pick[s], 5, outs[0] if s != t else None, outs[-1], plan[t]["width"] ** 3)

    def cube(s):
        item = plan[s]
        rows, slot, width = item["rows"], item["slot"], item["width"]
        size = width**3
        cubes[s][...] = jnp.zeros(cubes[s].shape, jnp.float32)
        for q in range(width**2):
            cubes[s][q * slot : q * slot + rows, :size] = states[s][:, q * size : (q + 1) * size]

    def scalar(key, kind, mode, a, b):
        return scalars[((combos[key] * 2 + kind) * 2 + mode) * 64 + a * 8 + b]

    def self_part(s):
        item = plan[s]
        slot, width = item["slot"], item["width"]
        size = width**3
        total = totals[s]
        total[:, :size] = dot3(split(cubes[s][:, :size]), split(tails[(s, s)][0][:, :size]), ((1,), (0,)))
        block = width * slot
        for tile in range(-(-size // lanes)):
            at = slice(tile * lanes, (tile + 1) * lanes)

            @pl.loop(0, width)
            def _(i):
                base = pl.multiple_of(i * block, 8)
                held = [cubes[s][pl.ds(base + b * slot, slot), at] for b in range(width)]
                for a in range(width):
                    out = total[pl.ds(base + a * slot, slot), at]
                    for b in range(width):
                        out = out + scalar((s, s), 1, 1, a, b) * held[b]
                    total[pl.ds(base + a * slot, slot), at] = out

            @pl.loop(0, width)
            def _(i):
                base = pl.multiple_of(i * slot, 8)
                held = [cubes[s][pl.ds(base + b * block, slot), at] for b in range(width)]
                for a in range(width):
                    out = total[pl.ds(base + a * block, slot), at]
                    for b in range(width):
                        out = out + scalar((s, s), 1, 0, a, b) * held[b]
                    total[pl.ds(base + a * block, slot), at] = out

    def self_density(s):
        item = plan[s]
        slot, width = item["slot"], item["width"]
        size = width**3
        data = split(cubes[s][:, :size])
        gram = None
        step = width * slot
        dims = (((0,), (0,)), ((), ()))
        gram = lax.dot_general(data[0], data[0], dims, preferred_element_type=jnp.float32) + 2.0 * lax.dot_general(
            data[0], data[1], dims, preferred_element_type=jnp.float32
        )
        for k in range(3):
            add_density(
                s, 5 + k, gram, tail_rest_turned[s][:, k : k + 1], tail_rest[s][k : k + 1, :], tail_pick[s][k], tail_turned[s][k]
            )
        column = lax.broadcasted_iota(jnp.int32, (8, 8), 1)
        wide_lanes = cubes[s].shape[1]
        rows_of_sums[...] = jnp.zeros(rows_of_sums.shape, jnp.float32)
        for mode in range(2):
            block = jnp.zeros((8, 8), jnp.float32)
            for i in range(width):
                for j in range(width):
                    row = None
                    for other in range(width):
                        left = (i * width + other if mode == 0 else other * width + i) * slot
                        right = (j * width + other if mode == 0 else other * width + j) * slot
                        term = cubes[s][left : left + slot, :] * cubes[s][right : right + slot, :]
                        row = term if row is None else row + term
                    rows_of_sums[j : j + 1, :wide_lanes] = jnp.sum(row, axis=0, keepdims=True)
                column_sum = jnp.sum(rows_of_sums[:, :wide_lanes], axis=1, keepdims=True)
                block = jnp.where(column == i, column_sum, block)
            put_density(s, 3 + mode, block)

    def pieces(t):
        item = plan[t]
        tiles, columns, size = item["tiles"], item["columns"], item["width"] ** 3
        out = []
        for at_place in range(wide):
            for tile in range(tiles):
                start = (at_place * tiles + tile) * lanes
                stop = min(start + lanes, columns)
                while start < stop:
                    q = start // size
                    end = min(stop, (q + 1) * size)
                    out.append((at_place, tile, start % lanes, end - start, q, start - q * size, start))
                    start = end
        return out

    def wait_home(t):
        keep_home(t).wait()
        for step in range(1, wide):
            home(t, step).wait_recv()

    def take_action(t):
        item = plan[t]
        rows, tiles = item["rows"], item["tiles"]
        for at_place in range(wide):
            for tile in range(tiles):
                start = (at_place * tiles + tile) * lanes
                width = min(lanes, item["columns"] - start)
                if width > 0:
                    stepped[t][:, start : start + width] = back[t][at_place, tile * rows : (tile + 1) * rows, :width]

    def pair_part(s, t):
        item = plan[t]
        rows, slot = plan[s]["rows"], plan[s]["slot"]
        wide_in, wide_out, size = item["width"], plan[s]["width"], item["width"] ** 3
        offset = item["rows"] * item["tiles"]
        if s > t and t > 0:
            offset += 2 * plan[t - 1]["rows"] * item["tiles"]
        listed = pieces(t)
        for target in (zero_in, one_in):
            for at_place, tile, lane, length, q, inside, _ in listed:
                row = offset + tile * rows
                target[q * slot : q * slot + rows, inside : inside + length] = back[t][
                    at_place, row : row + rows, lane : lane + length
                ]
            offset += rows * item["tiles"]

        def stage_of(mode, loops, step, in_stride, out_stride, out_step, zero_from, one_from, zero_to, one_to):
            for tile in range(-(-size // lanes)):
                at = slice(tile * lanes, (tile + 1) * lanes)

                @pl.loop(0, loops)
                def _(i):
                    base = pl.multiple_of(i * step, 8)
                    out_base = pl.multiple_of(i * out_step, 8)
                    for group in range(0, slot, 8):
                        zero = [zero_from[pl.ds(base + b * in_stride + group, 8), at] for b in range(wide_in)]
                        one = [one_from[pl.ds(base + b * in_stride + group, 8), at] for b in range(wide_in)]
                        for a in range(wide_out):
                            next_zero, next_one = None, None
                            for b in range(wide_in):
                                over, pos = scalar((s, t), 0, mode, a, b), scalar((s, t), 1, mode, a, b)
                                zero_term, one_term = over * zero[b], over * one[b] + pos * zero[b]
                                next_zero = zero_term if b == 0 else next_zero + zero_term
                                next_one = one_term if b == 0 else next_one + one_term
                            zero_to[pl.ds(out_base + a * out_stride + group, 8), at] = next_zero
                            one_to[pl.ds(out_base + a * out_stride + group, 8), at] = next_one

        stage_of(1, wide_in, wide_in * slot, slot, slot, wide_out * slot, zero_in, one_in, zero_out, one_out)
        stage_of(0, wide_out, slot, wide_out * slot, wide_out * slot, slot, zero_out, one_out, zero_in, one_in)
        live = wide_out**2 * slot
        out_size = wide_out**3
        over_tail, pos_tail = tails[(s, t)]
        totals[s][:, :out_size] += dot3(
            split(one_in[:live, :size]), split(over_tail[:, :out_size]), ((1,), (0,))
        ) + dot3(split(zero_in[:live, :size]), split(pos_tail[:, :out_size]), ((1,), (0,)))

    def finish(s):
        item = plan[s]
        rows, slot, size = item["rows"], item["slot"], item["width"] ** 3
        for q in range(item["width"] ** 2):
            at = slice(q * size, (q + 1) * size)
            stepped[s][:, at] = states[s][:, at] - time_step * (
                totals[s][q * slot : q * slot + rows, :size] + stepped[s][:, at]
            )

    def first_sum(step):
        return pltpu.make_async_remote_copy(
            src_ref=sums,
            dst_ref=stage.at[place],
            send_sem=sum_send.at[step],
            recv_sem=sum_recv.at[step],
            device_id=device(layer, peer(step)),
            device_id_type=mesh_ids,
        )

    def second_sum(step):
        return pltpu.make_async_remote_copy(
            src_ref=layer_sums.at[layer],
            dst_ref=layer_sums.at[layer],
            send_sem=sum_send.at[wide + step],
            recv_sem=sum_recv.at[wide + step],
            device_id=device(lax.rem(layer + step, layers), place),
            device_id_type=mesh_ids,
        )

    barrier = pltpu.get_barrier_semaphore()
    for step in range(1, wide):
        pl.semaphore_signal(barrier, inc=1, device_id=device(layer, peer(step)), device_id_type=mesh_ids)
    for step in range(1, layers):
        pl.semaphore_signal(
            barrier, inc=1, device_id=device(lax.rem(layer + step, layers), place), device_id_type=mesh_ids
        )
    pl.semaphore_wait(barrier, wide + layers - 2)

    hops = layers - 1
    early, late = 1, 0
    others = [t for t in range(count) if t not in (early, late)]
    for t in [early, late] + others:
        keep(t).start()
        for step in range(1, wide):
            across(t, step).start()

    def begin(t):
        layer_ready(t)
        forward(t, 0)

    def relay(t, step):
        arrive(t, step - 1)
        forward(t, step)

    begin(early)
    build_leads(early)
    for step in range(1, min(2, hops)):
        relay(early, step)
    begin(late)
    for step in range(2, hops):
        relay(early, step)
    for t in [late] + others:
        build_leads(t)
    arrive(early, hops - 1)
    mix(early)
    for t in others:
        begin(t)
    send_home(early)
    for s in range(count):
        cube(s)
        build_tail(s, s)
    relay(late, 1)
    for s in range(count):
        for t in (s - 1, s + 1):
            if 0 <= t < count:
                build_tail(s, t)
    for s in range(count):
        self_part(s)
    wait_home(early)
    take_action(early)
    pair_part(0, early)
    for step in range(2, hops):
        relay(late, step)
    for t in others:
        relay(t, 1)
    pair_part(2, early)
    for s in range(count):
        self_density(s)
    for t in others:
        for step in range(2, hops):
            relay(t, step)
    arrive(late, hops - 1)
    mix(late)
    last = late
    for t in others:
        arrive(t, hops - 1)
        mix(t)
        send_home(last)
        last = t
    for step in range(1, wide):
        first_sum(step).start()
    stage[place] = sums[...]
    send_home(last)
    for t in [late] + others:
        wait_home(t)
        take_action(t)
        for s in (t - 1, t + 1):
            if 0 <= s < count:
                pair_part(s, t)
        if t == late:
            for step in range(1, wide):
                first_sum(step).wait()
            layer_sums[layer] = jnp.sum(stage[...], axis=0)
        if t == others[0]:
            for step in range(1, layers):
                second_sum(step).start()
    for s in range(count):
        finish(s)
    for step in range(1, layers):
        second_sum(step).wait()
    whole = jnp.sum(layer_sums[...], axis=0)
    for t in range(count):
        width = plan[t]["width"]
        for mode in range(8):
            at = (t * 8 + mode) * 8
            densities[t][mode] = whole[:width, at : at + width] * (1.0 / float(width**7))

    for t in range(count):
        for step in range(1, wide):
            across(t, step).wait_send()
            home(t, step).wait_send()
        for step in range(hops):
            for up in (True, False):
                @pl.when(sends_hop(step, up))
                def _():
                    hop(t, step, up).wait_send()


def call(kernel, outs, scratch, *args, name, remote=None):
    extra = params
    if remote is not None:
        extra = pltpu.CompilerParams(vmem_limit_bytes=vmem_limit, collective_id=remote, has_side_effects=True)
    return pl.pallas_call(
        kernel,
        out_shape=[jax.ShapeDtypeStruct(shape, jnp.float32) for shape in outs],
        in_specs=[pl.BlockSpec(memory_space=pltpu.SMEM) if arg.ndim == 1 else vmem for arg in args],
        out_specs=[vmem] * len(outs),
        scratch_shapes=[pltpu.VMEM(shape, jnp.float32) if isinstance(shape, tuple) else shape for shape in scratch],
        compiler_params=extra,
        name=name,
    )(*args)


def round_up(value, unit):
    return -(-value // unit) * unit


def spread(table, rows, slot):
    shape = table.shape[:-1]
    held = table.reshape(shape + (-1, rows))
    wider = np.full(shape + (held.shape[-2], slot), -1 if table.dtype == np.int32 else 0, table.dtype)
    wider[..., :rows] = held
    return wider.reshape(shape + (-1,))


def local(*args):
    states = args[:4]
    operators = args[4:8]
    intersections, positions, coupling_pair, coupling_mode, coupling_strength = args[8:]
    devices = lax.axis_size("grp") * lax.axis_size("sub")
    count = len(states)
    widths = [operator.shape[1] for operator in operators]
    rows = [state.shape[0] for state in states]
    columns = [state.shape[1] for state in states]
    totals = [size * devices for size in rows]
    layers = max(1, lax.axis_size("grp") // 4)
    wide = devices // layers
    tiles = [-(-size // (wide * lanes)) for size in columns]
    slots = [round_up(size, 8) for size in rows]
    pairs, modes = intersections.shape[:2]

    sends = call(
        functools.partial(pack_kernel, [(rows[s], columns[s], tiles[s]) for s in range(count)]),
        [(wide, round_up(rows[s] * tiles[s], 8), lanes) for s in range(count)],
        [],
        *states,
        name="pack",
    )

    pair_pick = (coupling_pair[:, None] == jnp.arange(pairs, dtype=jnp.int32)[None, :]).astype(jnp.float32)
    mode_pick = (coupling_mode[:, None] == jnp.arange(modes, dtype=jnp.int32)[None, :]).astype(jnp.float32)
    weight_table = jnp.sum(
        coupling_strength[:, None, None] * pair_pick[:, :, None] * mode_pick[:, None, :], axis=0
    )
    both = jnp.stack([intersections, weight_table[:, :, None, None] * positions])

    def square(cut):
        return jnp.pad(cut, ((0, 0), (0, 0), (0, 8 - cut.shape[2]), (0, 8 - cut.shape[3])))

    combos = {}
    small = []
    for p in range(pairs):
        cut = both[:, p, :, : widths[p], : widths[p + 1]]
        for key, item in (((p, p + 1), cut), ((p + 1, p), jnp.swapaxes(cut, 2, 3))):
            combos[key] = len(small)
            small.append(square(item))
    for s in range(count):
        unit = jnp.broadcast_to(jnp.eye(widths[s], dtype=jnp.float32), operators[s].shape)
        turned = jnp.concatenate([operators[s][:5], jnp.swapaxes(operators[s][5:], 1, 2)])
        combos[(s, s)] = len(small)
        small.append(square(jnp.stack([unit, turned])))
    small = jnp.stack(small)
    scalars = small[:, :, 3:5].reshape(-1)
    small = small.reshape(-1, 8, 8)

    order = [[(t, "pos")] + [(s, kind) for s in (t - 1, t + 1) if 0 <= s < count for kind in ("over", "pos")] for t in range(count)]
    kinds = list(dict.fromkeys(zip(widths, rows)))
    plan = [
        dict(
            rows=rows[t],
            slot=slots[t],
            tiles=tiles[t],
            columns=columns[t],
            width=widths[t],
            kind=kinds.index((widths[t], rows[t])),
            targets=[rows[s] for s, kind in order[t]],
        )
        for t in range(count)
    ]
    back_shapes = [(wide, round_up(sum(item["targets"]) * item["tiles"], 8), lanes) for item in plan]
    tables = {name: [] for name in ("pick", "turned", "rest", "rest_turned")}
    for lead in (True, False):
        for width, held in kinds:
            size = held * devices if lead else width**3
            pick = np.zeros((3, 8, size), np.float32)
            rest = np.stack([others(width, 3, size, place) for place in range(3)])
            for place in range(3):
                pick[place, :width] = digits(width, 3, size, place)
            if lead:
                rest, pick = spread(rest, held, round_up(held, 8)), spread(pick, held, round_up(held, 8))
            tables["pick"].append(jnp.asarray(pick))
            tables["turned"].append(jnp.asarray(np.ascontiguousarray(pick.transpose(0, 2, 1))))
            tables["rest"].append(jnp.asarray(rest))
            tables["rest_turned"].append(jnp.asarray(np.ascontiguousarray(rest.T)))
    names = ("pick", "turned", "rest", "rest_turned")
    constants = [item for name in names for item in tables[name][: len(kinds)]] + [
        item for name in names for item in tables[name][len(kinds) :]
    ]
    cube_shapes = [(widths[s] ** 2 * slots[s], round_up(widths[s] ** 3, lanes)) for s in range(count)]
    mixed_shape = (max(widths) ** 2 * max(slots), round_up(max(widths) ** 3, lanes))
    depths = [devices * slots[t] for t in range(count)]
    dma = pltpu.SemaphoreType.DMA
    sum_shape = (8, count * 64)
    flowed = call(
        functools.partial(flow_kernel, plan, combos, layers, wide),
        [state.shape for state in states] + [(modes, widths[t], widths[t]) for t in range(count)],
        [(layers,) + send.shape for send in sends]
        + back_shapes * 2
        + [(max(depths), max(tiles) * lanes), (wide * max(rows), 2 * lanes)]
        + [(wide * rows[s], depths[t]) for t in range(count) for s, kind in order[t]]
        + [(widths[t] ** 3, round_up(widths[s] ** 3, lanes)) for s, t in combos for _ in range(1 if s == t else 2)]
        + cube_shapes * 2
        + [mixed_shape] * 4
        + [(round_up(max(widths) ** 2, 8), max(depths + [mixed_shape[1]]))] * 2
        + [(max(totals), max(depths))] * 2
        + [sum_shape, (wide,) + sum_shape, (layers,) + sum_shape, (8, mixed_shape[1])]
        + [dma((count, wide))] * 2
        + [dma((count, layers))] * 4
        + [dma((count, wide))] * 2
        + [dma((2 * count,))]
        + [dma((wide + layers,))] * 2,
        *sends,
        *states,
        small,
        scalars,
        *constants,
        name="flow",
        remote=0,
    )
    return tuple(flowed)


def solution(mesh):
    sharded = P(("grp", "sub"), None)
    return jax.shard_map(
        local,
        mesh=mesh,
        in_specs=(sharded,) * 4 + (P(),) * 9,
        out_specs=(sharded,) * 4 + (P(),) * 4,
        check_vma=False,
    )
```

profile of v0, /device:TPU:0, one launch (start us, length us, event | category | flops | bytes accessed | tf_op | source)
XLA Modules:
  0.0 185.0 jit_solution(6752933376034031159)
XLA Ops:
  0.6 0.0 copy-start
  0.6 0.7 fusion.10
  1.4 0.7 fusion.6
  2.0 0.1 multiply_reduce_fusion
  2.1 0.7 slice_bitcast_fusion.3
  2.9 0.7 slice_bitcast_fusion.2
  3.6 0.7 slice_bitcast_fusion.1
  4.3 0.8 slice_bitcast_fusion
  5.1 0.9 copy.94
  6.0 0.9 copy.93
  6.9 0.9 copy.92
  7.8 0.9 copy.91
  8.7 1.0 multiply_bitcast_fusion
  9.6 0.7 pad_maximum_fusion.2
  10.4 0.2 copy.76
  10.6 0.0 copy-done
  10.6 0.1 copy.81
  10.8 0.1 copy.82
  11.0 0.1 slice.52
  11.1 1.1 copy.83
  12.2 0.1 copy.84
  12.3 0.7 reshape.82.refs_9_
  13.1 2.5 %pack.1 = (f32[8,192,128]{2,1,0:T(8,128)}, f32[8,56,128]{2,1,0:T(8,128)}, f32[8,56,128]{2,1,0:T(8,128)}, f32[8,16,128]{2,1,0:T(8,128)}) custom-call(f32[11,16807]{1,0:T(8,128)} %refs_4_.1, f32[7,7776]{1,0:T(8,128)} %refs_5_.1, f32[7,7776]{1,0:T(8,128)} %refs_6_.1, f32[4,3125]{1,0:T(4,128)} %refs_7_.1), custom_call_target="tpu_custom_call" | custom-call | tf_op jit(solution)/shard_map/pack/pallas_call | solution.py:585
  15.6 159.6 %flow.1 = (f32[11,16807]{1,0:T(8,128)}, f32[7,7776]{1,0:T(8,128)}, f32[7,7776]{1,0:T(8,128)}, f32[4,3125]{1,0:T(4,128)}, f32[8,7,7]{2,1,0:T(8,128)}, /*index=5*/...) custom-call(f32[8,192,128]{2,1,0:T(8,128)} %get-tuple-element.12.refs_0_, ...), custom_call_target="tpu_custom_call" | custom-call | tf_op jit(solution)/shard_map/flow/pallas_call | solution.py:585
  175.1 1.4 copy.88
  176.5 1.4 copy.86
  177.9 1.4 copy.87
  179.2 1.4 copy.85
  180.6 0.0 copy-start.2
  180.6 0.0 copy-start.1
  180.6 0.0 copy-start.3
  180.6 2.3 %copy.108 = f32[11,16807]{1,0:T(8,128)} copy(f32[11,16807]{1,0:T(8,128)} %get-tuple-element.56) | data formatting | bytes 1479016
  183.0 0.0 copy-done.2
  183.0 0.7 copy.109
  183.7 0.0 copy-done.1
  183.7 0.7 copy.110
  184.4 0.0 copy-done.3
  184.4 0.6 copy.111
  (24 shorter events, 0.2 us)
Async XLA Ops:
  0.6 10.0 %copy-start = (f32[3,8,7,7]{3,1,2,0:T(8,128)S(1)}, f32[3,8,7,7]{3,1,2,0:T(8,128)}, u32[]{:S(2)}) copy-start(f32[3,8,7,7]{3,1,2,0:T(8,128)} %param.45) | copy-start | bytes 14116
  180.6 2.4 %copy-start.2 = (f32[7,7776]{1,0:T(8,128)S(1)}, f32[7,7776]{1,0:T(8,128)}, u32[]{:S(2)}) copy-start(f32[7,7776]{1,0:T(8,128)} %get-tuple-element.57) | copy-start | bytes 653188
  180.6 3.0 %copy-start.1 = (f32[7,7776]{1,0:T(8,128)S(1)}, f32[7,7776]{1,0:T(8,128)}, u32[]{:S(2)}) copy-start(f32[7,7776]{1,0:T(8,128)} %get-tuple-element.58) | copy-start | bytes 653188
  180.6 3.7 %copy-start.3 = (f32[4,3125]{1,0:T(4,128)S(1)}, f32[4,3125]{1,0:T(4,128)}, u32[]{:S(2)}) copy-start(f32[4,3125]{1,0:T(4,128)} %get-tuple-element.59) | copy-start | bytes 150004
where the time goes:
time: 186 us; the launch traced here: 185 us
  Pallas kernels  162 us (87%)
  local copies, waits for them, and re-layouts  18.8 us (10%)
  other arithmetic  3.29 us (2%)
    pallas_call x2, Pallas kernels, call(): pl.pallas_call(kernel, out_shape=[jax.ShapeDtypeStruct(shape, jnp.float32...  162 us
    unnamed x24, local copies, waits for them, and re-layouts  7.92 us
    pallas_call x4, local copies, waits for them, and re-layouts, call(): pl.pallas_call(kernel, out_shape=[jax.ShapeDtypeStruct(shape, jnp.float32...  5.48 us

commit v1 on v0

--- a/solution.py
+++ b/solution.py
@@ -43,16 +43,19 @@
     return go(left[0], right[0]) + (go(left[0], right[1]) + go(left[1], right[0]))
 
 
-def pack_kernel(plan, *refs):
+def pack_kernel(plan, chunks, *refs):
     count = len(plan)
-    for source, out, (rows, columns, tiles) in zip(refs[:count], refs[count:], plan):
-        used = tiles * rows
+    sources = refs[:count]
+    for out, (t, first, number) in zip(refs[count:], chunks):
+        source, item = sources[t], plan[t]
+        rows = item["rows"]
+        used = number * rows
         if out.shape[1] > used:
             out[:, used:, :] = jnp.zeros((out.shape[0], out.shape[1] - used, lanes), jnp.float32)
         for device in range(out.shape[0]):
-            for tile in range(tiles):
-                start = (device * tiles + tile) * lanes
-                width = min(lanes, columns - start)
+            for tile in range(number):
+                start = (device * item["tiles"] + first + tile) * lanes
+                width = min(lanes, item["columns"] - start)
                 at = slice(tile * rows, (tile + 1) * rows)
                 if width < lanes:
                     out[device, at, :] = jnp.zeros((rows, lanes), jnp.float32)
@@ -60,7 +63,19 @@
                     out[device, at, :width] = source[:, start : start + width]
 
 
-def flow_kernel(plan, combos, layers, wide, *refs):
+def finish_kernel(count, *refs):
+    states, changes, sums = refs[:count], refs[count : 2 * count], refs[2 * count]
+    stepped, densities = refs[2 * count + 1 : 3 * count + 1], refs[3 * count + 1 :]
+    for state, change, out in zip(states, changes, stepped):
+        out[...] = state[...] - time_step * change[...]
+    for t, out in enumerate(densities):
+        width, modes = out.shape[:2]
+        for mode in range(modes):
+            at = (t * 8 + mode) * 8
+            out[:, mode, :] = sums[:width, at : at + width] * (1.0 / float(width ** (modes - 1)))
+
+
+def flow_kernel(plan, chunks, combos, layers, wide, *refs):
     count = len(plan)
     spare = list(refs)
 
@@ -69,22 +84,26 @@
         del spare[:number]
         return taken
 
-    sends, states = take(count), take(count)
-    small, scalars = take(2)
+    parts = len(chunks)
+    sends, states = take(parts), take(count)
+    intersections, positions = take(2)
+    operators = take(count)
+    (coupling,) = take(1)
     kinds = [item["kind"] for item in plan]
     tables = [take(max(kinds) + 1) for _ in range(8)]
     lead_pick, lead_turned, lead_rest, lead_rest_turned, tail_pick, tail_turned, tail_rest, tail_rest_turned = [
         [table[kind] for kind in kinds] for table in tables
     ]
-    stepped, densities = take(count), take(count)
-    gathered, mixed, back = take(count), take(count), take(count)
+    changes = take(count)
+    (sums_out,) = take(1)
+    gathered, mixed, back = take(parts), take(parts), take(parts)
     value, result = take(2)
     matrices = [take(len(item["targets"])) for item in plan]
     tails = {key: take(1 if key[0] == key[1] else 2) for key in combos}
     cubes, totals = take(count), take(count)
     zero_in, one_in, zero_out, one_out = take(4)
     inner_over, inner_pos, full_over, full_pos = take(4)
-    sums, stage, layer_sums, rows_of_sums = take(4)
+    small, splats, sums, stage, layer_sums, rows_of_sums = take(6)
     across_send, across_recv, up_send, up_recv, down_send, down_recv, home_send, home_recv, own, sum_send, sum_recv = spare
 
     sub = lax.axis_size("sub")
@@ -167,18 +186,18 @@
         return pltpu.make_async_copy(sends[t].at[place], gathered[t].at[layer, place], own.at[t])
 
     def keep_home(t):
-        return pltpu.make_async_copy(mixed[t].at[place], back[t].at[place], own.at[count + t])
+        return pltpu.make_async_copy(mixed[t].at[place], back[t].at[place], own.at[parts + t])
 
     def layer_ready(t):
         keep(t).wait()
         for step in range(1, wide):
             across(t, step).wait_recv()
 
-    def put_density(t, mode, block):
+    def put_density(more, t, mode, block):
         at = (t * 8 + mode) * 8
-        sums[:, at : at + 8] = block
-
-    def add_density(t, mode, gram, rest_rows, rest_columns, pick, turned):
+        sums[:, at : at + 8] = sums[:, at : at + 8] + block if more else block
+
+    def add_density(more, t, mode, gram, rest_rows, rest_columns, pick, turned):
         kept = split(jnp.where(rest_rows == rest_columns, gram, 0.0))
         chosen = pick.astype(jnp.bfloat16)
         dims = (((1,), (1,)), ((), ()))
@@ -188,11 +207,12 @@
         block = lax.dot_general(
             turned, right, (((0,), (0,)), ((), ())), precision=highest, preferred_element_type=jnp.float32
         )
-        put_density(t, mode, 0.5 * (block + block.T))
-
-    def mix(t):
+        put_density(more, t, mode, 0.5 * (block + block.T))
+
+    def mix(c):
+        t, first, tiles = chunks[c]
         item = plan[t]
-        rows, slot, tiles = item["rows"], item["slot"], item["tiles"]
+        rows, slot = item["rows"], item["slot"]
         depth = layers * wide * slot
         value[:depth, : tiles * lanes] = jnp.zeros((depth, tiles * lanes), jnp.float32)
 
@@ -202,7 +222,7 @@
             def _(at_place):
                 base = pl.multiple_of((at_layer * wide + at_place) * slot, slot)
                 for tile in range(tiles):
-                    value[pl.ds(base, rows), tile * lanes : (tile + 1) * lanes] = gathered[t][
+                    value[pl.ds(base, rows), tile * lanes : (tile + 1) * lanes] = gathered[c][
                         at_layer, at_place, tile * rows : (tile + 1) * rows, :
                     ]
 
@@ -229,15 +249,15 @@
                 for at_place in range(wide):
                     for tile in range(wide_tiles):
                         row = offset + (start + tile) * target
-                        mixed[t][at_place, row : row + target, :] = result[
+                        mixed[c][at_place, row : row + target, :] = result[
                             at_place * target : (at_place + 1) * target, tile * lanes : (tile + 1) * lanes
                         ]
                 offset += target * tiles
-        if mixed[t].shape[1] > offset:
-            mixed[t][:, offset:, :] = jnp.zeros((wide, mixed[t].shape[1] - offset, lanes), jnp.float32)
+        if mixed[c].shape[1] > offset:
+            mixed[c][:, offset:, :] = jnp.zeros((wide, mixed[c].shape[1] - offset, lanes), jnp.float32)
         for k in range(3):
             turned = lead_turned[t][k, mine, :]
-            add_density(t, k, gram, lead_rest_turned[t][mine, k : k + 1], lead_rest[t][k : k + 1, :], lead_pick[t][k], turned)
+            add_density(first > 0, t, k, gram, lead_rest_turned[t][mine, k : k + 1], lead_rest[t][k : k + 1, :], lead_pick[t][k], turned)
 
     def send_home(t):
         keep_home(t).start()
@@ -299,7 +319,42 @@
             cubes[s][q * slot : q * slot + rows, :size] = states[s][:, q * size : (q + 1) * size]
 
     def scalar(key, kind, mode, a, b):
-        return scalars[((combos[key] * 2 + kind) * 2 + mode) * 64 + a * 8 + b]
+        row = ((combos[key] * 2 + kind) * 2 + mode) * 64 + b * 8 + a
+        return splats[row : row + 1, :]
+
+    def prepare():
+        small[...] = jnp.zeros(small.shape, jnp.float32)
+        pair, mode_of, strength = coupling[0:1, :], coupling[1:2, :], coupling[2:3, :]
+        for p in range(count - 1):
+            rows, cols = plan[p]["width"], plan[p + 1]["width"]
+            for k in range(8):
+                chosen = jnp.logical_and(pair == float(p), mode_of == float(k))
+                weight = jnp.sum(jnp.where(chosen, strength, 0.0), axis=1, keepdims=True)
+                for kind, source in enumerate((intersections, positions)):
+                    block = source[p, :rows, k, :cols]
+                    if kind:
+                        block = weight * block
+                    at = (combos[(p, p + 1)] * 2 + kind) * 8 + k
+                    small[at, :rows, :cols] = block
+                    small[(combos[(p + 1, p)] * 2 + kind) * 8 + k] = small[at].T
+        row = lax.broadcasted_iota(jnp.int32, (8, 8), 0)
+        column = lax.broadcasted_iota(jnp.int32, (8, 8), 1)
+        for t in range(count):
+            width = plan[t]["width"]
+            unit = jnp.where(jnp.logical_and(row == column, row < width), 1.0, 0.0)
+            for k in range(8):
+                small[combos[(t, t)] * 16 + k] = unit
+                at = combos[(t, t)] * 16 + 8 + k
+                small[at, :width, :width] = operators[t][:, k, :]
+                if k >= 5:
+                    small[at] = small[at].T
+        for key in combos:
+            for kind in range(2):
+                for mode in range(2):
+                    matrix = small[(combos[key] * 2 + kind) * 8 + 3 + mode]
+                    base = ((combos[key] * 2 + kind) * 2 + mode) * 64
+                    for b in range(8):
+                        splats[base + b * 8 : base + b * 8 + 8, :] = jnp.broadcast_to(matrix[:, b : b + 1], (8, lanes))
 
     def self_part(s):
         item = plan[s]
@@ -344,7 +399,7 @@
         )
         for k in range(3):
             add_density(
-                s, 5 + k, gram, tail_rest_turned[s][:, k : k + 1], tail_rest[s][k : k + 1, :], tail_pick[s][k], tail_turned[s][k]
+                False, s, 5 + k, gram, tail_rest_turned[s][:, k : k + 1], tail_rest[s][k : k + 1, :], tail_pick[s][k], tail_turned[s][k]
             )
         column = lax.broadcasted_iota(jnp.int32, (8, 8), 1)
         wide_lanes = cubes[s].shape[1]
@@ -362,53 +417,63 @@
                     rows_of_sums[j : j + 1, :wide_lanes] = jnp.sum(row, axis=0, keepdims=True)
                 column_sum = jnp.sum(rows_of_sums[:, :wide_lanes], axis=1, keepdims=True)
                 block = jnp.where(column == i, column_sum, block)
-            put_density(s, 3 + mode, block)
-
-    def pieces(t):
-        item = plan[t]
-        tiles, columns, size = item["tiles"], item["columns"], item["width"] ** 3
+            put_density(False, s, 3 + mode, block)
+
+    def pieces(c):
+        t, first, tiles = chunks[c]
+        columns, size = plan[t]["columns"], plan[t]["width"] ** 3
         out = []
         for at_place in range(wide):
             for tile in range(tiles):
-                start = (at_place * tiles + tile) * lanes
+                start = (at_place * plan[t]["tiles"] + first + tile) * lanes
                 stop = min(start + lanes, columns)
                 while start < stop:
                     q = start // size
                     end = min(stop, (q + 1) * size)
-                    out.append((at_place, tile, start % lanes, end - start, q, start - q * size, start))
+                    out.append((at_place, tile, start % lanes, end - start, q, start - q * size))
                     start = end
         return out
 
-    def wait_home(t):
-        keep_home(t).wait()
+    def wait_home(c):
+        keep_home(c).wait()
         for step in range(1, wide):
-            home(t, step).wait_recv()
-
-    def take_action(t):
+            home(c, step).wait_recv()
+
+    def flat(s):
+        item = plan[s]
+        rows, slot, size = item["rows"], item["slot"], item["width"] ** 3
+        for q in range(item["width"] ** 2):
+            changes[s][:, q * size : (q + 1) * size] = totals[s][q * slot : q * slot + rows, :size]
+
+    def add_action(c):
+        t, first, tiles = chunks[c]
         item = plan[t]
-        rows, tiles = item["rows"], item["tiles"]
+        rows = item["rows"]
         for at_place in range(wide):
             for tile in range(tiles):
-                start = (at_place * tiles + tile) * lanes
+                start = (at_place * item["tiles"] + first + tile) * lanes
                 width = min(lanes, item["columns"] - start)
                 if width > 0:
-                    stepped[t][:, start : start + width] = back[t][at_place, tile * rows : (tile + 1) * rows, :width]
+                    changes[t][:, start : start + width] += back[c][at_place, tile * rows : (tile + 1) * rows, :width]
 
     def pair_part(s, t):
         item = plan[t]
         rows, slot = plan[s]["rows"], plan[s]["slot"]
         wide_in, wide_out, size = item["width"], plan[s]["width"], item["width"] ** 3
-        offset = item["rows"] * item["tiles"]
+        before = item["rows"]
         if s > t and t > 0:
-            offset += 2 * plan[t - 1]["rows"] * item["tiles"]
-        listed = pieces(t)
-        for target in (zero_in, one_in):
-            for at_place, tile, lane, length, q, inside, _ in listed:
-                row = offset + tile * rows
-                target[q * slot : q * slot + rows, inside : inside + length] = back[t][
-                    at_place, row : row + rows, lane : lane + length
-                ]
-            offset += rows * item["tiles"]
+            before += 2 * plan[t - 1]["rows"]
+        for c, chunk in enumerate(chunks):
+            if chunk[0] != t:
+                continue
+            offset = before * chunk[2]
+            for target in (zero_in, one_in):
+                for at_place, tile, lane, length, q, inside in pieces(c):
+                    row = offset + tile * rows
+                    target[q * slot : q * slot + rows, inside : inside + length] = back[c][
+                        at_place, row : row + rows, lane : lane + length
+                    ]
+                offset += rows * chunk[2]
 
         def stage_of(mode, loops, step, in_stride, out_stride, out_step, zero_from, one_from, zero_to, one_to):
             for tile in range(-(-size // lanes)):
@@ -440,15 +505,6 @@
             split(one_in[:live, :size]), split(over_tail[:, :out_size]), ((1,), (0,))
         ) + dot3(split(zero_in[:live, :size]), split(pos_tail[:, :out_size]), ((1,), (0,)))
 
-    def finish(s):
-        item = plan[s]
-        rows, slot, size = item["rows"], item["slot"], item["width"] ** 3
-        for q in range(item["width"] ** 2):
-            at = slice(q * size, (q + 1) * size)
-            stepped[s][:, at] = states[s][:, at] - time_step * (
-                totals[s][q * slot : q * slot + rows, :size] + stepped[s][:, at]
-            )
-
     def first_sum(step):
         return pltpu.make_async_remote_copy(
             src_ref=sums,
@@ -479,103 +535,128 @@
     pl.semaphore_wait(barrier, wide + layers - 2)
 
     hops = layers - 1
-    early, late = 1, 0
-    others = [t for t in range(count) if t not in (early, late)]
-    for t in [early, late] + others:
-        keep(t).start()
+    of = [[c for c in range(parts) if chunks[c][0] == t] for t in range(count)]
+    early, late = of[1], of[0]
+    rest = [c for t in range(2, count) for c in of[t]]
+    for c in early + late + rest:
+        keep(c).start()
         for step in range(1, wide):
-            across(t, step).start()
-
-    def begin(t):
-        layer_ready(t)
-        forward(t, 0)
-
-    def relay(t, step):
-        arrive(t, step - 1)
-        forward(t, step)
-
-    begin(early)
-    build_leads(early)
-    for step in range(1, min(2, hops)):
-        relay(early, step)
-    begin(late)
-    for step in range(2, hops):
-        relay(early, step)
-    for t in [late] + others:
-        build_leads(t)
-    arrive(early, hops - 1)
-    mix(early)
-    for t in others:
-        begin(t)
-    send_home(early)
+            across(c, step).start()
+
+    def begin(c):
+        layer_ready(c)
+        forward(c, 0)
+
+    def relay(c, step):
+        if step < hops:
+            arrive(c, step - 1)
+            forward(c, step)
+
+    def relays(some, steps):
+        for step in steps:
+            for c in some:
+                relay(c, step)
+
+    def gathered_now(some):
+        if hops:
+            for c in some:
+                arrive(c, hops - 1)
+
+    prepare()
+    for c in early:
+        begin(c)
+    build_leads(1)
+    for c in late[:1]:
+        begin(c)
+    relays(early, (1,))
+    for c in late[1:]:
+        begin(c)
+    for t in range(count):
+        if t != 1:
+            build_leads(t)
+    relays(late[:1], (1,))
+    relays(early, (2,))
     for s in range(count):
         cube(s)
+    relays(late[1:], (1,))
+    relays(early, range(3, hops))
+    for s in range(count):
         build_tail(s, s)
-    relay(late, 1)
+    self_part(0)
+    relays(late[:1], (2,))
+    gathered_now(early)
+    for c in early:
+        mix(c)
+    relays(late[1:], (2,))
+    for c in early:
+        send_home(c)
+    for c in rest:
+        begin(c)
+    relays(late, range(3, hops))
     for s in range(count):
         for t in (s - 1, s + 1):
             if 0 <= t < count:
                 build_tail(s, t)
-    for s in range(count):
+    self_density(0)
+    for c in late:
+        gathered_now([c])
+        mix(c)
+        relays(rest, (1,) if c == late[0] else ())
+        send_home(c)
+    for s in range(1, count):
         self_part(s)
-    wait_home(early)
-    take_action(early)
-    pair_part(0, early)
-    for step in range(2, hops):
-        relay(late, step)
-    for t in others:
-        relay(t, 1)
-    pair_part(2, early)
-    for s in range(count):
+    relays(rest, range(2, hops))
+    for c in early:
+        wait_home(c)
+    pair_part(0, 1)
+    for s in range(1, count):
         self_density(s)
-    for t in others:
-        for step in range(2, hops):
-            relay(t, step)
-    arrive(late, hops - 1)
-    mix(late)
-    last = late
-    for t in others:
-        arrive(t, hops - 1)
-        mix(t)
-        send_home(last)
-        last = t
+    gathered_now(rest)
+    for c in rest:
+        mix(c)
     for step in range(1, wide):
         first_sum(step).start()
     stage[place] = sums[...]
-    send_home(last)
-    for t in [late] + others:
-        wait_home(t)
-        take_action(t)
+    for c in rest:
+        send_home(c)
+    pair_part(2, 1)
+    flat(0)
+    for c in late:
+        wait_home(c)
+    for c in late:
+        add_action(c)
+    pair_part(1, 0)
+    for step in range(1, wide):
+        first_sum(step).wait()
+    layer_sums[layer] = jnp.sum(stage[...], axis=0)
+    for t in range(2, count):
+        for c in of[t]:
+            wait_home(c)
         for s in (t - 1, t + 1):
             if 0 <= s < count:
                 pair_part(s, t)
-        if t == late:
-            for step in range(1, wide):
-                first_sum(step).wait()
-            layer_sums[layer] = jnp.sum(stage[...], axis=0)
-        if t == others[0]:
+        if t == 2:
             for step in range(1, layers):
                 second_sum(step).start()
-    for s in range(count):
-        finish(s)
+        flat(t - 1)
+        for c in of[t - 1]:
+            add_action(c)
+    flat(count - 1)
+    for c in of[count - 1]:
+        add_action(c)
     for step in range(1, layers):
         second_sum(step).wait()
-    whole = jnp.sum(layer_sums[...], axis=0)
-    for t in range(count):
-        width = plan[t]["width"]
-        for mode in range(8):
-            at = (t * 8 + mode) * 8
-            densities[t][mode] = whole[:width, at : at + width] * (1.0 / float(width**7))
-
-    for t in range(count):
+    sums_out[...] = jnp.sum(layer_sums[...], axis=0)
+
+    for c in range(parts):
         for step in range(1, wide):
-            across(t, step).wait_send()
-            home(t, step).wait_send()
+            across(c, step).wait_send()
+            home(c, step).wait_send()
         for step in range(hops):
             for up in (True, False):
                 @pl.when(sends_hop(step, up))
                 def _():
-                    hop(t, step, up).wait_send()
+                    hop(c, step, up).wait_send()
 
 
 def call(kernel, outs, scratch, *args, name, remote=None):
@@ -585,7 +666,7 @@
     return pl.pallas_call(
         kernel,
         out_shape=[jax.ShapeDtypeStruct(shape, jnp.float32) for shape in outs],
-        in_specs=[pl.BlockSpec(memory_space=pltpu.SMEM) if arg.ndim == 1 else vmem for arg in args],
+        in_specs=[vmem] * len(args),
         out_specs=[vmem] * len(outs),
         scratch_shapes=[pltpu.VMEM(shape, jnp.float32) if isinstance(shape, tuple) else shape for shape in scratch],
         compiler_params=extra,
@@ -621,39 +702,12 @@
     slots = [round_up(size, 8) for size in rows]
     pairs, modes = intersections.shape[:2]
 
-    sends = call(
-        functools.partial(pack_kernel, [(rows[s], columns[s], tiles[s]) for s in range(count)]),
-        [(wide, round_up(rows[s] * tiles[s], 8), lanes) for s in range(count)],
-        [],
-        *states,
-        name="pack",
-    )
-
-    pair_pick = (coupling_pair[:, None] == jnp.arange(pairs, dtype=jnp.int32)[None, :]).astype(jnp.float32)
-    mode_pick = (coupling_mode[:, None] == jnp.arange(modes, dtype=jnp.int32)[None, :]).astype(jnp.float32)
-    weight_table = jnp.sum(
-        coupling_strength[:, None, None] * pair_pick[:, :, None] * mode_pick[:, None, :], axis=0
-    )
-    both = jnp.stack([intersections, weight_table[:, :, None, None] * positions])
-
-    def square(cut):
-        return jnp.pad(cut, ((0, 0), (0, 0), (0, 8 - cut.shape[2]), (0, 8 - cut.shape[3])))
-
     combos = {}
-    small = []
     for p in range(pairs):
-        cut = both[:, p, :, : widths[p], : widths[p + 1]]
-        for key, item in (((p, p + 1), cut), ((p + 1, p), jnp.swapaxes(cut, 2, 3))):
-            combos[key] = len(small)
-            small.append(square(item))
+        combos[(p, p + 1)] = len(combos)
+        combos[(p + 1, p)] = len(combos)
     for s in range(count):
-        unit = jnp.broadcast_to(jnp.eye(widths[s], dtype=jnp.float32), operators[s].shape)
-        turned = jnp.concatenate([operators[s][:5], jnp.swapaxes(operators[s][5:], 1, 2)])
-        combos[(s, s)] = len(small)
-        small.append(square(jnp.stack([unit, turned])))
-    small = jnp.stack(small)
-    scalars = small[:, :, 3:5].reshape(-1)
-    small = small.reshape(-1, 8, 8)
+        combos[(s, s)] = len(combos)
 
     order = [[(t, "pos")] + [(s, kind) for s in (t - 1, t + 1) if 0 <= s < count for kind in ("over", "pos")] for t in range(count)]
     kinds = list(dict.fromkeys(zip(widths, rows)))
@@ -669,7 +723,22 @@
         )
         for t in range(count)
     ]
-    back_shapes = [(wide, round_up(sum(item["targets"]) * item["tiles"], 8), lanes) for item in plan]
+    chunks = []
+    for t in range(count):
+        cut = -(-tiles[t] // 2) if t == 0 else tiles[t]
+        for first in range(0, tiles[t], cut):
+            chunks.append((t, first, min(cut, tiles[t] - first)))
+    sends = call(
+        functools.partial(pack_kernel, plan, chunks),
+        [(wide, round_up(rows[t] * number, 8), lanes) for t, first, number in chunks],
+        [],
+        *states,
+        name="pack",
+    )
+    back_shapes = [(wide, round_up(sum(plan[t]["targets"]) * number, 8), lanes) for t, first, number in chunks]
+    coupling = jnp.stack(
+        [coupling_pair.astype(jnp.float32), coupling_mode.astype(jnp.float32), coupling_strength]
+    )
     tables = {name: [] for name in ("pick", "turned", "rest", "rest_turned")}
     for lead in (True, False):
         for width, held in kinds:
@@ -694,32 +763,43 @@
     dma = pltpu.SemaphoreType.DMA
     sum_shape = (8, count * 64)
     flowed = call(
-        functools.partial(flow_kernel, plan, combos, layers, wide),
-        [state.shape for state in states] + [(modes, widths[t], widths[t]) for t in range(count)],
+        functools.partial(flow_kernel, plan, chunks, combos, layers, wide),
+        [state.shape for state in states] + [sum_shape],
         [(layers,) + send.shape for send in sends]
         + back_shapes * 2
-        + [(max(depths), max(tiles) * lanes), (wide * max(rows), 2 * lanes)]
+        + [(max(depths), max(number for t, first, number in chunks) * lanes), (wide * max(rows), 2 * lanes)]
         + [(wide * rows[s], depths[t]) for t in range(count) for s, kind in order[t]]
         + [(widths[t] ** 3, round_up(widths[s] ** 3, lanes)) for s, t in combos for _ in range(1 if s == t else 2)]
         + cube_shapes * 2
         + [mixed_shape] * 4
         + [(round_up(max(widths) ** 2, 8), max(depths + [mixed_shape[1]]))] * 2
         + [(max(totals), max(depths))] * 2
+        + [(len(combos) * 16, 8, 8), (len(combos) * 256, lanes)]
         + [sum_shape, (wide,) + sum_shape, (layers,) + sum_shape, (8, mixed_shape[1])]
-        + [dma((count, wide))] * 2
-        + [dma((count, layers))] * 4
-        + [dma((count, wide))] * 2
-        + [dma((2 * count,))]
+        + [dma((len(chunks), wide))] * 2
+        + [dma((len(chunks), layers))] * 4
+        + [dma((len(chunks), wide))] * 2
+        + [dma((2 * len(chunks),))]
         + [dma((wide + layers,))] * 2,
         *sends,
         *states,
-        small,
-        scalars,
+        jnp.transpose(intersections, (0, 2, 1, 3)),
+        jnp.transpose(positions, (0, 2, 1, 3)),
+        *[jnp.transpose(operator, (1, 0, 2)) for operator in operators],
+        coupling,
         *constants,
         name="flow",
         remote=0,
     )
-    return tuple(flowed)
+    finished = call(
+        functools.partial(finish_kernel, count),
+        [state.shape for state in states] + [(widths[t], modes, widths[t]) for t in range(count)],
+        [],
+        *states,
+        *flowed,
+        name="finish",
+    )
+    return tuple(finished[:count]) + tuple(jnp.transpose(item, (1, 0, 2)) for item in finished[count:])
 
 
 def solution(mesh):

time: 186 us -> 138 us (0.74)
  Pallas kernels: 162 us -> 135 us
  local copies, waits for them, and re-layouts: 18.8 us -> 0 us
    pallas_call x2 -> x3, Pallas kernels: 162 us -> 135 us  [call(): pl.pallas_call(kernel, out_shape=[jax.ShapeDtypeStruct(shape, jnp.float32...]
    unnamed x24 -> x0, local copies, waits for them, and re-layouts: 7.92 us -> none
    pallas_call x4 -> x0, local copies, waits for them, and re-layouts: 5.48 us -> none  [call(): pl.pallas_call(kernel, out_shape=[jax.ShapeDtypeStruct(shape, jnp.float32...]
    transpose x4 -> x0, local copies, waits for them, and re-layouts: 2.97 us -> none  [local(): jnp.swapaxes(operators[s][5:], 1, 2)]
where the time goes in v1:
time: 138 us
  Pallas kernels  135 us (98%)
  other arithmetic  1.92 us (1%)
    pallas_call x3, Pallas kernels, call(): pl.pallas_call(kernel, out_shape=[jax.ShapeDtypeStruct(shape, jnp.float32...  135 us

profile of v1, /device:TPU:0, one launch (start us, length us, event | category | flops | bytes accessed | tf_op | source)
XLA Modules:
  0.0 138.0 jit_solution(8149870853565663223)
XLA Ops:
  0.6 0.7 convert_bitcast_fusion
  1.3 1.2 pad_maximum_fusion.refs_15_
  2.5 2.5 %pack.1 = (f32[8,104,128]{2,1,0:T(8,128)}, f32[8,88,128]{2,1,0:T(8,128)}, f32[8,56,128]{2,1,0:T(8,128)}, f32[8,56,128]{2,1,0:T(8,128)}, f32[8,16,128]{2,1,0:T(8,128)}) custom-call(f32[11,16807]{1,0:T(8,128)} %refs_0_.3, f32[7,7776]{1,0:T(8,128)} %refs_1_.3, f32[7,7776]{1,0:T(8,128)} %refs_2_.3, f32[4,3125]{1,0:T(4,128)} %refs_3_.3), custom_call_target="tpu_custom_call" | custom-call | tf_op jit(solution)/shard_map/pack/pallas_call | solution.py:666
  5.0 129.4 %flow.1 = (f32[11,16807]{1,0:T(8,128)}, f32[7,7776]{1,0:T(8,128)}, f32[7,7776]{1,0:T(8,128)}, f32[4,3125]{1,0:T(4,128)}, f32[8,256]{1,0:T(8,128)}) custom-call(f32[8,104,128]{2,1,0:T(8,128)} %get-tuple-element.26.refs_0_, f32[8,88,128]{2,1,0:T(8,128)} %get-tuple-element.27.refs_1_, f32[8,56,128]{2,1,0:T(8,128)} %get-tuple-element.28.refs_2_, ...), custom_call_target="tpu_custom_call" | custom-call | tf_op jit(solution)/shard_map/flow/pallas_call | solution.py:666
  134.4 3.5 %finish.1 = (f32[11,16807]{1,0:T(8,128)}, f32[7,7776]{1,0:T(8,128)}, f32[7,7776]{1,0:T(8,128)}, f32[4,3125]{1,0:T(4,128)}, f32[7,8,7]{2,1,0:T(8,128)}, /*index=5...) custom-call(f32[11,16807]{1,0:T(8,128)} %refs_0_.3, f32[7,7776]{1,0:T(8,128)} %refs_1_.3, f32[7,7776]{1,0:T(8,128)} %refs_2_.3, ...), custom_call_target="tpu_custom_call" | custom-call | tf_op jit(solution)/shard_map/finish/pallas_call | solution.py:666

commit v2 on v1

--- a/solution.py
+++ b/solution.py
@@ -536,9 +536,8 @@
 
     hops = layers - 1
     of = [[c for c in range(parts) if chunks[c][0] == t] for t in range(count)]
-    early, late = of[1], of[0]
-    rest = [c for t in range(2, count) for c in of[t]]
-    for c in early + late + rest:
+    line = of[3] + of[1] + of[2] + of[0]
+    for c in line:
         keep(c).start()
         for step in range(1, wide):
             across(c, step).start()
@@ -552,98 +551,86 @@
             arrive(c, step - 1)
             forward(c, step)
 
-    def relays(some, steps):
-        for step in steps:
-            for c in some:
-                relay(c, step)
-
-    def gathered_now(some):
-        if hops:
-            for c in some:
+    def local_begin(stage_at):
+        if stage_at == 0:
+            prepare()
+            build_leads(3)
+            build_leads(1)
+        elif stage_at == 1:
+            build_leads(2)
+            build_leads(0)
+        elif stage_at == 2:
+            for s in range(count):
+                cube(s)
+                build_tail(s, s)
+                for t in (s - 1, s + 1):
+                    if 0 <= t < count:
+                        build_tail(s, t)
+
+    def close(s):
+        flat(s)
+        for c in of[s]:
+            add_action(c)
+
+    def local_after(c):
+        if c in of[3]:
+            self_part(0)
+        elif c in of[1]:
+            for s in range(1, count):
+                self_part(s)
+        elif c in of[2]:
+            self_density(0)
+        elif c == of[0][0]:
+            for s in range(1, count):
+                self_density(s)
+
+    def collect(c):
+        t = chunks[c][0]
+        wait_home(c)
+        if t:
+            for s in (t - 1, t + 1):
+                if 0 <= s < count:
+                    pair_part(s, t)
+
+    arrived = []
+    for at in range(max(len(line) + hops, 3)):
+        if at < len(line):
+            begin(line[at])
+        for step in range(1, hops):
+            if 0 <= at - step < len(line):
+                relay(line[at - step], step)
+        local_begin(at)
+        if at >= hops and at - hops < len(line):
+            c = line[at - hops]
+            if len(arrived) >= 3 and c != line[-1]:
+                collect(arrived.pop(0))
+            if hops:
                 arrive(c, hops - 1)
-
-    prepare()
-    for c in early:
-        begin(c)
-    build_leads(1)
-    for c in late[:1]:
-        begin(c)
-    relays(early, (1,))
-    for c in late[1:]:
-        begin(c)
-    for t in range(count):
-        if t != 1:
-            build_leads(t)
-    relays(late[:1], (1,))
-    relays(early, (2,))
-    for s in range(count):
-        cube(s)
-    relays(late[1:], (1,))
-    relays(early, range(3, hops))
-    for s in range(count):
-        build_tail(s, s)
-    self_part(0)
-    relays(late[:1], (2,))
-    gathered_now(early)
-    for c in early:
-        mix(c)
-    relays(late[1:], (2,))
-    for c in early:
-        send_home(c)
-    for c in rest:
-        begin(c)
-    relays(late, range(3, hops))
-    for s in range(count):
-        for t in (s - 1, s + 1):
-            if 0 <= t < count:
-                build_tail(s, t)
-    self_density(0)
-    for c in late:
-        gathered_now([c])
-        mix(c)
-        relays(rest, (1,) if c == late[0] else ())
-        send_home(c)
-    for s in range(1, count):
-        self_part(s)
-    relays(rest, range(2, hops))
-    for c in early:
-        wait_home(c)
-    pair_part(0, 1)
-    for s in range(1, count):
-        self_density(s)
-    gathered_now(rest)
-    for c in rest:
-        mix(c)
-    for step in range(1, wide):
-        first_sum(step).start()
-    stage[place] = sums[...]
-    for c in rest:
-        send_home(c)
-    pair_part(2, 1)
-    flat(0)
-    for c in late:
-        wait_home(c)
-    for c in late:
-        add_action(c)
-    pair_part(1, 0)
-    for step in range(1, wide):
-        first_sum(step).wait()
-    layer_sums[layer] = jnp.sum(stage[...], axis=0)
-    for t in range(2, count):
-        for c in of[t]:
-            wait_home(c)
-        for s in (t - 1, t + 1):
-            if 0 <= s < count:
-                pair_part(s, t)
-        if t == 2:
+            mix(c)
+            local_after(c)
+            if c == line[-1]:
+                for step in range(1, wide):
+                    first_sum(step).start()
+                stage[place] = sums[...]
+            send_home(c)
+            arrived.append(c)
+    done = []
+    for c in arrived:
+        if chunks[c][0] == 0 and not done:
+            flat(0)
+            close(2)
+            close(3)
+            for step in range(1, wide):
+                first_sum(step).wait()
+            layer_sums[layer] = jnp.sum(stage[...], axis=0)
             for step in range(1, layers):
                 second_sum(step).start()
-        flat(t - 1)
-        for c in of[t - 1]:
+            done.append(c)
+        collect(c)
+        if chunks[c][0] == 0:
             add_action(c)
-    flat(count - 1)
-    for c in of[count - 1]:
-        add_action(c)
+    pair_part(1, 0)
+    close(1)
     for step in range(1, layers):
         second_sum(step).wait()
     sums_out[...] = jnp.sum(layer_sums[...], axis=0)
@@ -725,9 +712,15 @@
     ]
     chunks = []
     for t in range(count):
-        cut = -(-tiles[t] // 2) if t == 0 else tiles[t]
-        for first in range(0, tiles[t], cut):
-            chunks.append((t, first, min(cut, tiles[t] - first)))
+        left, first = tiles[t], 0
+        while left:
+            number = -(-left // 2) if t == 0 and left == tiles[t] else left
+            if t == 0 and left == tiles[t] and number > 8:
+                number = 8
+            if t == 0 and first and left > 4:
+                number = -(-left // 2)
+            chunks.append((t, first, number))
+            first, left = first + number, left - number
     sends = call(
         functools.partial(pack_kernel, plan, chunks),
         [(wide, round_up(rows[t] * number, 8), lanes) for t, first, number in chunks],

time: 138 us -> 131 us (0.949)
  Pallas kernels: 135 us -> 128 us
    pallas_call x3, Pallas kernels: 135 us -> 128 us  [call(): pl.pallas_call(kernel, out_shape=[jax.ShapeDtypeStruct(shape, jnp.float32...]
where the time goes in v2:
time: 131 us; the launch traced here: 130 us
  Pallas kernels  128 us (98%)
  other arithmetic  1.92 us (1%)
    pallas_call x3, Pallas kernels, call(): pl.pallas_call(kernel, out_shape=[jax.ShapeDtypeStruct(shape, jnp.float32...  128 us

profile of v2, /device:TPU:0, one launch (start us, length us, event | category | flops | bytes accessed | tf_op | source)
XLA Modules:
  0.0 130.5 jit_solution(13953618686375603067)
XLA Ops:
  0.6 0.7 convert_bitcast_fusion
  1.3 1.2 pad_maximum_fusion.refs_16_
  2.5 2.5 %pack.1 = (f32[8,88,128]{2,1,0:T(8,128)}, f32[8,56,128]{2,1,0:T(8,128)}, f32[8,48,128]{2,1,0:T(8,128)}, f32[8,56,128]{2,1,0:T(8,128)}, f32[8,56,128]{2,1,0:T(8,128)}, /*index=5*/f32[8,16,128]{2,1,0:T(8,128)}) custom-call(f32[11,16807]{1,0:T(8,128)} %refs_0_.3, f32[7,7776]{1,0:T(8,128)} %refs_1_.3, f32[7,7776]{1,0:T(8,128)} %refs_2_.3, f32[4,3125]{1,0:T(4,128)} %refs_3_.3), custom_call_target="tpu_custom_call" | custom-call | tf_op jit(solution)/shard_map/pack/pallas_call | solution.py:653
  5.0 121.8 %flow.1 = (f32[11,16807]{1,0:T(8,128)}, f32[7,7776]{1,0:T(8,128)}, f32[7,7776]{1,0:T(8,128)}, f32[4,3125]{1,0:T(4,128)}, f32[8,256]{1,0:T(8,128)}) custom-call(f32[8,88,128]{2,1,0:T(8,128)} %get-tuple-element.27.refs_0_, f32[8,56,128]{2,1,0:T(8,128)} %get-tuple-element.28.refs_1_, f32[8,48,128]{2,1,0:T(8,128)} %get-tuple-element.29.refs_2_, ...), custom_call_target="tpu_custom_call" | custom-call | tf_op jit(solution)/shard_map/flow/pallas_call | solution.py:653
  126.9 3.5 %finish.1 = (f32[11,16807]{1,0:T(8,128)}, f32[7,7776]{1,0:T(8,128)}, f32[7,7776]{1,0:T(8,128)}, f32[4,3125]{1,0:T(4,128)}, f32[7,8,7]{2,1,0:T(8,128)}, /*index=5...) custom-call(f32[11,16807]{1,0:T(8,128)} %refs_0_.3, f32[7,7776]{1,0:T(8,128)} %refs_1_.3, f32[7,7776]{1,0:T(8,128)} %refs_2_.3, ...), custom_call_target="tpu_custom_call" | custom-call | tf_op jit(solution)/shard_map/finish/pallas_call | solution.py:653

commit v3 on v2

--- a/solution.py
+++ b/solution.py
@@ -15,6 +15,7 @@
 vmem_limit = 63 * 1024 * 1024
 params = pltpu.CompilerParams(vmem_limit_bytes=vmem_limit)
 vmem = pl.BlockSpec(memory_space=pltpu.VMEM)
+anywhere = pl.BlockSpec(memory_space=pl.ANY)
 mesh_ids = pl.DeviceIdType.MESH
 
 
@@ -85,15 +86,12 @@
         return taken
 
     parts = len(chunks)
-    sends, states = take(parts), take(count)
+    sends, states_far = take(parts), take(count)
     intersections, positions = take(2)
     operators = take(count)
-    (coupling,) = take(1)
+    coupling_pair, coupling_mode, coupling_strength = take(3)
     kinds = [item["kind"] for item in plan]
-    tables = [take(max(kinds) + 1) for _ in range(8)]
-    lead_pick, lead_turned, lead_rest, lead_rest_turned, tail_pick, tail_turned, tail_rest, tail_rest_turned = [
-        [table[kind] for kind in kinds] for table in tables
-    ]
+    tables_far = [take(max(kinds) + 1) for _ in range(8)]
     changes = take(count)
     (sums_out,) = take(1)
     gathered, mixed, back = take(parts), take(parts), take(parts)
@@ -104,7 +102,17 @@
     zero_in, one_in, zero_out, one_out = take(4)
     inner_over, inner_pos, full_over, full_pos = take(4)
     small, splats, sums, stage, layer_sums, rows_of_sums = take(6)
-    across_send, across_recv, up_send, up_recv, down_send, down_recv, home_send, home_recv, own, sum_send, sum_recv = spare
+    states = take(count)
+    tables_near = {which: take(max(kinds) + 1) for which in (1, 3, 5, 7)}
+    tables = [tables_near.get(which, table) for which, table in enumerate(tables_far)]
+    lead_pick, lead_turned, lead_rest, lead_rest_turned, tail_pick, tail_turned, tail_rest, tail_rest_turned = [
+        [table[kind] for kind in kinds] for table in tables
+    ]
+    loads = list(zip(states_far, states))
+    for which in tables_near:
+        loads += list(zip(tables_far[which], tables_near[which]))
+    across_send, across_recv, up_send, up_recv, down_send, down_recv, home_send, home_recv, own, sum_send, sum_recv, load = spare
+    fetches = [pltpu.make_async_copy(far, near, load.at[at]) for at, (far, near) in enumerate(loads)]
 
     sub = lax.axis_size("sub")
     me = lax.axis_index("grp") * sub + lax.axis_index("sub")
@@ -324,11 +332,11 @@
 
     def prepare():
         small[...] = jnp.zeros(small.shape, jnp.float32)
-        pair, mode_of, strength = coupling[0:1, :], coupling[1:2, :], coupling[2:3, :]
+        pair, mode_of, strength = coupling_pair[...], coupling_mode[...], coupling_strength[...]
         for p in range(count - 1):
             rows, cols = plan[p]["width"], plan[p + 1]["width"]
             for k in range(8):
-                chosen = jnp.logical_and(pair == float(p), mode_of == float(k))
+                chosen = jnp.logical_and(pair == p, mode_of == k)
                 weight = jnp.sum(jnp.where(chosen, strength, 0.0), axis=1, keepdims=True)
                 for kind, source in enumerate((intersections, positions)):
                     block = source[p, :rows, k, :cols]
@@ -525,6 +533,8 @@
             device_id_type=mesh_ids,
         )
 
+    for fetch in fetches:
+        fetch.start()
     barrier = pltpu.get_barrier_semaphore()
     for step in range(1, wide):
         pl.semaphore_signal(barrier, inc=1, device_id=device(layer, peer(step)), device_id_type=mesh_ids)
@@ -560,6 +570,8 @@
             build_leads(2)
             build_leads(0)
         elif stage_at == 2:
+            for fetch in fetches:
+                fetch.wait()
             for s in range(count):
                 cube(s)
                 build_tail(s, s)
@@ -592,7 +604,7 @@
                 if 0 <= s < count:
                     pair_part(s, t)
 
-    arrived = []
+    arrived, closed = [], []
     for at in range(max(len(line) + hops, 3)):
         if at < len(line):
             begin(line[at])
@@ -602,8 +614,13 @@
         local_begin(at)
         if at >= hops and at - hops < len(line):
             c = line[at - hops]
-            if len(arrived) >= 3 and c != line[-1]:
+            if len(arrived) >= 3:
                 collect(arrived.pop(0))
+            if c == line[-1] and not any(chunks[other][0] for other in arrived):
+                flat(0)
+                close(2)
+                close(3)
+                closed.append(c)
             if hops:
                 arrive(c, hops - 1)
             mix(c)
@@ -617,9 +634,10 @@
     done = []
     for c in arrived:
         if chunks[c][0] == 0 and not done:
-            flat(0)
-            close(2)
-            close(3)
+            if not closed:
+                flat(0)
+                close(2)
+                close(3)
             for step in range(1, wide):
                 first_sum(step).wait()
             layer_sums[layer] = jnp.sum(stage[...], axis=0)
@@ -646,16 +664,23 @@
                     hop(c, step, up).wait_send()
 
 
-def call(kernel, outs, scratch, *args, name, remote=None):
+def call(kernel, outs, scratch, *args, name, remote=None, far=()):
     extra = params
     if remote is not None:
         extra = pltpu.CompilerParams(vmem_limit_bytes=vmem_limit, collective_id=remote, has_side_effects=True)
     return pl.pallas_call(
         kernel,
         out_shape=[jax.ShapeDtypeStruct(shape, jnp.float32) for shape in outs],
-        in_specs=[vmem] * len(args),
+        in_specs=[anywhere if at in far else vmem for at in range(len(args))],
         out_specs=[vmem] * len(outs),
-        scratch_shapes=[pltpu.VMEM(shape, jnp.float32) if isinstance(shape, tuple) else shape for shape in scratch],
+        scratch_shapes=[
+            pltpu.VMEM(shape, jnp.float32)
+            if isinstance(shape, tuple)
+            else pltpu.VMEM(shape.shape, shape.dtype)
+            if isinstance(shape, jax.ShapeDtypeStruct)
+            else shape
+            for shape in scratch
+        ],
         compiler_params=extra,
         name=name,
     )(*args)
@@ -729,9 +754,6 @@
         name="pack",
     )
     back_shapes = [(wide, round_up(sum(plan[t]["targets"]) * number, 8), lanes) for t, first, number in chunks]
-    coupling = jnp.stack(
-        [coupling_pair.astype(jnp.float32), coupling_mode.astype(jnp.float32), coupling_strength]
-    )
     tables = {name: [] for name in ("pick", "turned", "rest", "rest_turned")}
     for lead in (True, False):
         for width, held in kinds:
@@ -755,6 +777,10 @@
     depths = [devices * slots[t] for t in range(count)]
     dma = pltpu.SemaphoreType.DMA
     sum_shape = (8, count * 64)
+    states_at = len(chunks)
+    tables_at = states_at + 2 * count + 5
+    far = set(range(states_at, states_at + count))
+    far |= {tables_at + at * len(kinds) + kind for at in (1, 3, 5, 7) for kind in range(len(kinds))}
     flowed = call(
         functools.partial(flow_kernel, plan, chunks, combos, layers, wide),
         [state.shape for state in states] + [sum_shape],
@@ -769,20 +795,30 @@
         + [(max(totals), max(depths))] * 2
         + [(len(combos) * 16, 8, 8), (len(combos) * 256, lanes)]
         + [sum_shape, (wide,) + sum_shape, (layers,) + sum_shape, (8, mixed_shape[1])]
+        + [state.shape for state in states]
+        + [
+            jax.ShapeDtypeStruct(constants[at * len(kinds) + kind].shape, constants[at * len(kinds) + kind].dtype)
+            for at in (1, 3, 5, 7)
+            for kind in range(len(kinds))
+        ]
         + [dma((len(chunks), wide))] * 2
         + [dma((len(chunks), layers))] * 4
         + [dma((len(chunks), wide))] * 2
         + [dma((2 * len(chunks),))]
-        + [dma((wide + layers,))] * 2,
+        + [dma((wide + layers,))] * 2
+        + [dma((count + 4 * len(kinds),))],
         *sends,
         *states,
         jnp.transpose(intersections, (0, 2, 1, 3)),
         jnp.transpose(positions, (0, 2, 1, 3)),
         *[jnp.transpose(operator, (1, 0, 2)) for operator in operators],
-        coupling,
+        coupling_pair[None, :],
+        coupling_mode[None, :],
+        coupling_strength[None, :],
         *constants,
         name="flow",
         remote=0,
+        far=far,
     )
     finished = call(
         functools.partial(finish_kernel, count),

time: 131 us -> 128 us (0.977)
  other arithmetic: 1.92 us -> 0 us
    another operation x2 -> x0, other arithmetic: 1.92 us -> none  [local(): jnp.stack([coupling_pair.astype(jnp.float32), coupling_mode.astype(jnp.fl...]
where the time goes in v3:
time: 128 us; the launch traced here: 127 us
  Pallas kernels  127 us (99%)
    pallas_call x3, Pallas kernels, call(): pl.pallas_call(kernel, out_shape=[jax.ShapeDtypeStruct(shape, jnp.float32...  127 us

profile of v3, /device:TPU:0, one launch (start us, length us, event | category | flops | bytes accessed | tf_op | source)
XLA Modules:
  0.0 127.3 jit_solution(5093362517699969972)
XLA Ops:
  0.6 2.5 %pack.1 = (f32[8,88,128]{2,1,0:T(8,128)}, f32[8,56,128]{2,1,0:T(8,128)}, f32[8,48,128]{2,1,0:T(8,128)}, f32[8,56,128]{2,1,0:T(8,128)}, f32[8,56,128]{2,1,0:T(8,128)}, /*index=5*/f32[8,16,128]{2,1,0:T(8,128)}) custom-call(f32[11,16807]{1,0:T(8,128)} %refs_0_.3, f32[7,7776]{1,0:T(8,128)} %refs_1_.3, f32[7,7776]{1,0:T(8,128)} %refs_2_.3, f32[4,3125]{1,0:T(4,128)} %refs_3_.3), custom_call_target="tpu_custom_call" | custom-call | tf_op jit(solution)/shard_map/pack/pallas_call | solution.py:671
  3.1 120.6 %flow.1 = (f32[11,16807]{1,0:T(8,128)}, f32[7,7776]{1,0:T(8,128)}, f32[7,7776]{1,0:T(8,128)}, f32[4,3125]{1,0:T(4,128)}, f32[8,256]{1,0:T(8,128)}) custom-call(f32[8,88,128]{2,1,0:T(8,128)} %get-tuple-element.27.refs_0_, f32[8,56,128]{2,1,0:T(8,128)} %get-tuple-element.28.refs_1_, f32[8,48,128]{2,1,0:T(8,128)} %get-tuple-element.29.refs_2_, ...), custom_call_target="tpu_custom_call" | custom-call | tf_op jit(solution)/shard_map/flow/pallas_call | solution.py:671
  123.7 3.5 %finish.1 = (f32[11,16807]{1,0:T(8,128)}, f32[7,7776]{1,0:T(8,128)}, f32[7,7776]{1,0:T(8,128)}, f32[4,3125]{1,0:T(4,128)}, f32[7,8,7]{2,1,0:T(8,128)}, /*index=5...) custom-call(f32[11,16807]{1,0:T(8,128)} %refs_0_.3, f32[7,7776]{1,0:T(8,128)} %refs_1_.3, f32[7,7776]{1,0:T(8,128)} %refs_2_.3, ...), custom_call_target="tpu_custom_call" | custom-call | tf_op jit(solution)/shard_map/finish/pallas_call | solution.py:671
